TPU v7x, 256 devices: a whole 4x4x8 slice. The times are simulated.
256 devices in a mesh: row: 16 (over z_hi, y), col: 16 (over z_lo, x, core).
Axes of the slice: x: 4, y: 4, z: 8 (z_hi: 4, z_lo: 2; z = z_hi * 2 + z_lo), core: 2. Of those that a mesh axis runs over, the one named last changes fastest.
Arguments:
- spectra: bfloat16 [4096, 128], P(('row', 'col')), may hold values from -6 to 6
- residual: bfloat16 [768, 128, 128, 128], P(('row', 'col')), may hold values from -1.5 to 1.5
- slot_tile: int32 [768], P(('row', 'col')), may hold values from -1 to 527, as said below
- tile_blocks: int32 [528, 2], replicated, may hold values from 0 to 31, as said below
Outputs:
- spectra_grad: float32 [4096, 128], P(('row', 'col'))
Inputs may be any that keep to these rules, and one draw needn't show every extreme that they name: `slot_tile`: every tile number appears in exactly one slot and all other slots hold -1. A tile with row block p and column block q sits on the device at mesh position (p mod 16, q mod 16), that is device number (p mod 16) * 16 + q mod 16 in the order of row+col. `tile_blocks`: row t holds the row block and the column block of tile t, the row block no larger than the column block; every such pair of blocks is exactly one tile.
All inputs are finite; a program needn't handle non-finite values.
Results may differ from a plain program's by a relative error of at most 0.004.
Values may be sent and summed in bfloat16 or wider, within the bound.
No kernel may reach another device: no remote copies, remote signals or barrier semaphores. Data moves between devices by JAX's collectives and lax.ppermute only.
A program may use at most 128 MiB of HBM per device.

v0:
```python
import math
import jax
import jax.numpy as jnp
from jax import lax
from jax.sharding import PartitionSpec as P


def dft_table(lag_count, freq_count):
    lag_index = jnp.arange(lag_count, dtype=jnp.int32) - lag_count // 2
    freq_index = jnp.arange(freq_count, dtype=jnp.int32)
    phase_steps = lag_index[:, None] * freq_index[None, :] % lag_count
    angles = phase_steps.astype(jnp.float32) * (2.0 * math.pi / lag_count)
    cosine = jnp.cos(angles) / lag_count
    sine = -jnp.sin(angles) / lag_count
    return jnp.concatenate([cosine, sine], axis=1).astype(jnp.bfloat16)


def pair_terms(spectral, row_spec, col_spec, freq_count):
    real_part = spectral[:, :, :freq_count]
    imag_part = spectral[:, :, freq_count:]
    row_re = row_spec[:, :freq_count].astype(jnp.float32)
    row_im = row_spec[:, freq_count:].astype(jnp.float32)
    col_re = col_spec[:, :freq_count].astype(jnp.float32)
    col_im = col_spec[:, freq_count:].astype(jnp.float32)
    row_gain_re = jnp.sum(real_part * col_re[None] - imag_part * col_im[None], axis=1)
    row_gain_im = jnp.sum(real_part * col_im[None] + imag_part * col_re[None], axis=1)
    col_gain_re = jnp.sum(real_part * row_re[:, None] + imag_part * row_im[:, None], axis=0)
    col_gain_im = jnp.sum(real_part * row_im[:, None] - imag_part * row_re[:, None], axis=0)
    row_gain = jnp.concatenate([row_gain_re, row_gain_im], axis=1)
    col_gain = jnp.concatenate([col_gain_re, col_gain_im], axis=1)
    return (row_gain, col_gain)


def block_major(flat, row_count, col_count, block_count, tile_size):
    per_row = block_count // row_count
    piece = tile_size // col_count
    grid = flat.reshape(row_count, col_count, per_row, piece, flat.shape[1])
    return jnp.transpose(grid, (2, 0, 1, 3, 4)).reshape(block_count, tile_size, flat.shape[1])


def station_major(blocks, row_count, col_count, block_count, tile_size):
    per_row = block_count // row_count
    piece = tile_size // col_count
    grid = blocks.reshape(per_row, row_count, col_count, piece, blocks.shape[2])
    return jnp.transpose(grid, (1, 2, 0, 3, 4)).reshape(block_count * tile_size, blocks.shape[2])


def add_block(gradient, contrib, index):
    current = lax.dynamic_index_in_dim(gradient, index, 0, keepdims=True)
    return lax.dynamic_update_index_in_dim(gradient, current + contrib[None], index, 0)


def on_device(spectra, residual, slot_tile, tile_blocks):
    slot_count, tile_size, _, lag_count = residual.shape
    freq_count = spectra.shape[1] // 2
    width = 2 * freq_count
    row_count = lax.axis_size("row")
    col_count = lax.axis_size("col")
    block_count = 2 * min(row_count, col_count)
    dft = dft_table(lag_count, freq_count)
    tile_total = tile_blocks.shape[0]
    matches = (slot_tile[:, None] == jnp.arange(tile_total, dtype=jnp.int32)[None, :]).astype(
        jnp.int32
    )
    chosen = jnp.sum(matches[:, :, None] * tile_blocks[None, :, :], axis=1)
    filled = slot_tile >= 0
    station_ids = jnp.arange(tile_size, dtype=jnp.int32)
    upper = station_ids[:, None] < station_ids[None, :]
    gathered = lax.all_gather(spectra, ("row", "col"), axis=0, tiled=True)
    row_source = block_major(gathered, row_count, col_count, block_count, tile_size)
    row_div = 1
    col_div = 1
    row_grad = jnp.zeros((row_source.shape[0], tile_size, width), jnp.float32)
    col_grad = jnp.zeros((row_source.shape[0], tile_size, width), jnp.float32)
    for slot_index in range(slot_count):
        row_block = chosen[slot_index, 0]
        col_block = chosen[slot_index, 1]
        pair_mask = (jnp.where(row_block == col_block, upper, True) & filled[slot_index]).astype(
            jnp.float32
        )
        tile_data = residual[slot_index]
        row_index = row_block // row_div
        col_index = col_block // col_div
        row_spec = lax.dynamic_index_in_dim(row_source, row_index, 0, keepdims=False)
        col_spec = lax.dynamic_index_in_dim(row_source, col_index, 0, keepdims=False)
        spectral = jnp.dot(
            tile_data.reshape(tile_size * tile_size, lag_count),
            dft,
            preferred_element_type=jnp.float32,
        )
        spectral = spectral.reshape(tile_size, tile_size, width) * pair_mask[:, :, None]
        row_gain, col_gain = pair_terms(spectral, row_spec, col_spec, freq_count)
        row_grad = add_block(row_grad, row_gain, row_index)
        col_grad = add_block(col_grad, col_gain, col_index)
    gradient = station_major(row_grad + col_grad, row_count, col_count, block_count, tile_size)
    return lax.psum_scatter(gradient, ("row", "col"), scatter_dimension=0, tiled=True)


def solution(mesh):
    return jax.shard_map(
        on_device,
        mesh=mesh,
        in_specs=(
            P(("row", "col"), None),
            P(("row", "col"), None, None, None),
            P(("row", "col")),
            P(),
        ),
        out_specs=P(("row", "col"), None),
        check_vma=False,
    )
```

profile of v0, /device:TPU:0, one launch (start us, length us, event | category | flops | bytes accessed | tf_op | source)
XLA Modules:
  0.0 1714.3 jit_solution(4478842264416761182)
XLA Ops:
  6.5 0.7 all-gather.2.cloned.1.call-update
  7.3 0.0 reduce-scatter.2.cloned.1.call-start
  7.3 0.7 fusion.25
  8.0 0.7 broadcast_compare_fusion
  8.7 0.8 multiply_reduce_fusion
  9.5 0.6 fusion.36
  10.1 0.7 fusion.37
  10.8 0.2 multiply_convert_fusion.1
  11.0 8.2 fusion.29
  19.1 4.5 convolution_bitcast_fusion.2
  23.6 4.5 convolution_bitcast_fusion.1
  28.1 4.5 convolution_bitcast_fusion
  33.7 0.6 fusion.14
  35.4 0.7 fusion.16
  44.6 8.2 copy.80
  52.9 8.2 copy.81
  61.1 4.7 copy.82
  69.4 0.6 fusion.18
  70.0 8.9 bitcast_multiply_fusion.2
  78.9 4.2 bitcast_multiply_fusion.1
  83.1 4.2 bitcast_multiply_fusion
  87.3 306.5 %all-gather.2.cloned.1.call-done = bf16[4096,128]{1,0:T(8,128)(2,1)} async-done(((bf16[16,128]{1,0:T(8,128)(2,1)}), bf16[4096,128]{1,0:T(8,128)(2,1)}) %all-gather.2.cloned.1.call-update) | async-done | bytes 1048592 | tf_op jit(solution)/shard_map/all_gather | solution.py:69
  393.8 1.5 copy.53
  395.4 0.1 fusion.34
  395.4 0.1 copy.68
  395.6 0.1 copy.69
  395.7 0.1 copy.74
  395.8 0.1 copy.75
  395.9 0.1 fusion.32
  396.0 0.1 copy.70
  396.1 0.1 copy.71
  396.2 0.1 copy.76
  396.3 0.1 copy.77
  396.4 0.1 fusion.30
  396.5 0.1 copy.72
  396.6 0.1 copy.73
  396.7 0.1 copy.78
  396.8 0.1 copy.79
  397.0 8.5 add_reduce_fusion.2
  405.5 0.2 broadcast.110.clone.1
  405.8 5.2 add_reduce_fusion.1
  411.0 5.2 add_reduce_fusion
  416.2 0.2 broadcast.110.clone
  416.6 0.3 add.106
  416.8 1.9 copy.66
  418.7 3.1 copy.67
  421.8 0.0 reduce-scatter.2.cloned.1.call-update
  421.8 1285.6 %reduce-scatter.2.cloned.1.call-done = f32[16,128]{1,0:T(8,128)} async-done(((f32[4096,128]{1,0:T(8,128)}), f32[16,128]{1,0:T(8,128)}) %reduce-scatter.2.cloned.1.call-update) | async-done | bytes 8208 | tf_op jit(solution)/shard_map/reduce_scatter | solution.py:96
  (40 shorter events, 0.2 us)
Async XLA Ops:
  6.5 387.3 %all-gather.2.cloned.1.call-start = ((), (), s32[]{:S(2)}) async-start(), calls=%async_computation.1 | async-start | bytes 1052672 | tf_op jit(solution)/shard_map/all_gather | solution.py:69
  7.3 1700.2 %reduce-scatter.2.cloned.1.call-start = ((), (), s32[]{:S(2)}) async-start(), calls=%async_computation.2 | async-start | bytes 2105344 | tf_op jit(solution)/shard_map/reduce_scatter | solution.py:96
  44.6 16.4 slice-start.4
  52.9 8.2 slice-start.5
  70.0 8.9 copy-start.1
  70.0 13.1 slice-start.2
  78.9 4.2 slice-start.3
  396.9 8.8 copy-start
  397.0 14.0 slice-start
  405.5 5.5 slice-start.1
Sparse Core Ops, SparseCore 0:
  9.1 384.6 all-gather.1
  421.9 1285.4 reduce-scatter.1
where the time goes:
time: 1710 us
  waiting for transfers between devices  1590 us (93%)
  other arithmetic  40.8 us (2%)
  local copies, waits for them, and re-layouts  38.9 us (2%)
  between operations  28.2 us (2%)
    reduce_scatter x1, waiting for transfers between devices, on_device(): lax.psum_scatter(gradient, ('row', 'col'), scatter_dimension=0, tiled=True)  1290 us
    all_gather x1, waiting for transfers between devices, on_device(): gathered = lax.all_gather(spectra, ('row', 'col'), axis=0, tiled=True)  307 us
  transfers between devices with their start and end apart: 2, of which 2 were waited for; matrix products, arithmetic and copies ran while one was open for 4% of the time, Pallas kernels for 0%

commit v1 on v0

--- a/solution.py
+++ b/solution.py
@@ -66,7 +66,10 @@
     filled = slot_tile >= 0
     station_ids = jnp.arange(tile_size, dtype=jnp.int32)
     upper = station_ids[:, None] < station_ids[None, :]
-    gathered = lax.all_gather(spectra, ("row", "col"), axis=0, tiled=True)
+    gathered = jnp.concatenate(
+        lax.all_to_all(jnp.stack([spectra] * lax.axis_size(("row", "col"))), ("row", "col"), 0, 0),
+        axis=0,
+    )
     row_source = block_major(gathered, row_count, col_count, block_count, tile_size)
     row_div = 1
     col_div = 1

time: 1710 us -> 1430 us (0.84)
  waiting for transfers between devices: 1590 us -> 1290 us
    all_gather x1 -> x0, waiting for transfers between devices: 307 us -> none  [on_device(): gathered = lax.all_gather(spectra, ('row', 'col'), axis=0, tiled=True)]
  transfers between devices with their start and end apart: 2 -> 2, of which waited for: 2 -> 1; matrix products, arithmetic and copies ran while one was open for 4% -> 5% of each run, Pallas kernels for 0% -> 0%
where the time goes in v1:
time: 1430 us
  waiting for transfers between devices  1290 us (90%)
  other arithmetic  40.9 us (3%)
  local copies, waits for them, and re-layouts  39.6 us (3%)
  between operations  28.2 us (2%)
  starting transfers between devices  14.6 us (1%)
    reduce_scatter x1, waiting for transfers between devices, on_device(): lax.psum_scatter(gradient, ('row', 'col'), scatter_dimension=0, tiled=True)  1290 us
  transfers between devices with their start and end apart: 2, of which 1 were waited for; matrix products, arithmetic and copies ran while one was open for 5% of the time, Pallas kernels for 0%

profile of v1, /device:TPU:0, one launch (start us, length us, event | category | flops | bytes accessed | tf_op | source)
XLA Modules:
  0.0 1428.7 jit_solution(10225532969479599324)
XLA Ops:
  6.5 1.8 stack.2
  8.3 14.6 %all-to-all-start = ((bf16[256,16,128]{2,1,0:T(8,128)(2,1)}), bf16[256,16,128]{2,1,0:T(8,128)(2,1)S(1)}, u32[]{:S(2)}, u32[]{:S(2)}) async-start(bf16[256,16,128]{2,1,0:T(8,128)(2,1)} %stack.2), calls=%async_computation | async-start | bytes 2097152 | tf_op jit(solution)/shard_map/all_to_all | solution.py:70
  22.9 0.0 reduce-scatter.2.cloned.1.call-start
  23.0 0.7 fusion.25
  23.7 0.7 broadcast_compare_fusion
  24.4 0.8 multiply_reduce_fusion
  25.2 0.6 fusion.36
  25.8 0.7 fusion.37
  26.5 0.2 multiply_convert_fusion.1
  26.6 8.4 fusion.29
  35.0 4.5 convolution_bitcast_fusion.2
  39.5 4.5 convolution_bitcast_fusion.1
  43.9 4.5 convolution_bitcast_fusion
  49.5 0.6 fusion.14
  51.3 0.7 fusion.16
  60.5 8.2 copy.81
  68.7 8.2 copy.82
  76.9 4.7 copy.83
  85.2 0.6 fusion.18
  85.9 8.9 bitcast_multiply_fusion.2
  94.8 4.2 bitcast_multiply_fusion.1
  99.0 4.2 bitcast_multiply_fusion
  103.1 0.3 copy.54
  103.5 0.1 fusion.34
  103.5 0.1 copy.69
  103.7 0.1 copy.70
  103.8 0.1 copy.75
  103.9 0.1 copy.76
  104.0 0.1 fusion.32
  104.1 0.1 copy.71
  104.2 0.1 copy.72
  104.3 0.1 copy.77
  104.4 0.1 copy.78
  104.5 0.1 fusion.30
  104.6 0.1 copy.73
  104.7 0.1 copy.74
  104.8 0.1 copy.79
  104.9 0.1 copy.80
  105.1 8.6 add_reduce_fusion.2
  113.7 0.2 broadcast.112.clone.1
  113.9 5.2 add_reduce_fusion.1
  119.2 5.2 add_reduce_fusion
  124.4 0.2 broadcast.112.clone
  124.7 0.3 add.106
  124.9 1.9 copy.67
  126.8 3.1 copy.68
  129.9 0.0 reduce-scatter.2.cloned.1.call-update
  129.9 1291.9 %reduce-scatter.2.cloned.1.call-done = f32[16,128]{1,0:T(8,128)} async-done(((f32[4096,128]{1,0:T(8,128)}), f32[16,128]{1,0:T(8,128)}) %reduce-scatter.2.cloned.1.call-update) | async-done | bytes 8208 | tf_op jit(solution)/shard_map/reduce_scatter | solution.py:99
  (40 shorter events, 0.2 us)
Async XLA Ops:
  8.3 94.8 %all-to-all-start = ((bf16[256,16,128]{2,1,0:T(8,128)(2,1)}), bf16[256,16,128]{2,1,0:T(8,128)(2,1)S(1)}, u32[]{:S(2)}, u32[]{:S(2)}) async-start(bf16[256,16,128]{2,1,0:T(8,128)(2,1)} %stack.2), calls=%async_computation | async-start | bytes 2097152 | tf_op jit(solution)/shard_map/all_to_all | solution.py:70
  22.9 1398.9 %reduce-scatter.2.cloned.1.call-start = ((), (), s32[]{:S(2)}) async-start(), calls=%async_computation.2 | async-start | bytes 2105344 | tf_op jit(solution)/shard_map/reduce_scatter | solution.py:99
  60.5 16.4 %slice-start.4 = ((s8[8388608]{0:T(1024)(128)(4,1)}), s8[4194304]{0:T(1024)(128)(4,1)S(1)}, s32[]{:S(2)}) async-start(s8[8388608]{0:T(1024)(128)(4,1)} %bitcast.92), calls=%async_computation.7 | async-start | bytes 8388608
  68.7 8.2 slice-start.5
  85.9 8.9 copy-start.1
  85.9 13.1 slice-start.2
  94.8 4.2 slice-start.3
  105.0 8.9 copy-start
  105.1 14.1 slice-start
  113.7 5.5 slice-start.1
Sparse Core Ops, SparseCore 0:
  130.0 1291.7 reduce-scatter.1
